TPU v7x, 256 devices: a whole 4x4x8 slice. The times are simulated.
256 devices in a mesh: row: 32 (over x, z), col: 8 (over y, core).
Axes of the slice: x: 4, y: 4, z: 8, core: 2. Of those that a mesh axis runs over, the one named last changes fastest.
Arguments:
- kernel: float32 [2048, 65536], P('row', 'col'), may hold values from -6 to 6
- basis: float32 [65536, 128], P('col', 'row'), may hold values from -0.0234375 to 0.0234375
- responses: float32 [2048, 512], P('row', 'col'), may hold values from -6 to 6
Outputs:
- scores: float32 [2048, 128], P('row')
- loadings: float32 [128, 65536], P('row', 'col')
- weights: float32 [512, 128], P('col')
- deflated: float32 [2048, 65536], P('row', 'col')
- basis_next: float32 [2048, 128], P('row')
All inputs are finite; a program needn't handle non-finite values.
Results may differ from a plain program's by a relative error of at most 0.00012.
Values sent between devices are 32-bit elements; how exact they have to be, the bound alone decides.
No kernel may reach another device: no remote copies, remote signals or barrier semaphores. Data moves between devices by JAX's collectives and lax.ppermute only.
A program may use at most 64 MiB of HBM per device.

v0:
```python
import math
import jax
import jax.numpy as jnp
from jax import lax
from jax.sharding import Mesh
from jax.sharding import PartitionSpec as P

ROW = ("row_0", "row_1")


def sent_to_all(x, axis):
    devices = lax.axis_size(axis)
    return lax.all_to_all(jnp.broadcast_to(x[None], (devices, *x.shape)), axis, 0, 0, tiled=True)


def taken_together(x, axis):
    everything = sent_to_all(x, axis)
    return jnp.sum(everything, axis=0)


def summed_rows(subtotal, axes):
    for axis in axes:
        subtotal = lax.psum_scatter(subtotal, axis, scatter_dimension=0, tiled=True)
    return subtotal


def local(kernel, basis, responses):
    highest = lax.Precision.HIGHEST
    row_count = kernel.shape[0] * lax.axis_size(ROW)
    resp_count = responses.shape[1] * lax.axis_size("col")
    root_rows = math.sqrt(row_count)
    partial_proj = jnp.dot(
        kernel, lax.all_gather(basis, ROW, axis=1, tiled=True), precision=highest
    )
    projected = taken_together(partial_proj, "col")
    gram_part = jnp.dot(projected.T, projected, precision=highest) / row_count
    gram_mat = taken_together(gram_part, ROW)
    factor = jnp.linalg.cholesky(gram_mat)
    scores = jax.scipy.linalg.solve_triangular(factor, projected.T, lower=True).T
    weight_part = jnp.dot(responses.T, scores, precision=highest) / root_rows
    weights = taken_together(weight_part, ROW)
    next_part = jnp.dot(responses, weights, precision=highest) / math.sqrt(resp_count)
    basis_next = taken_together(next_part, "col")
    loadings = summed_rows(jnp.dot(scores.T, kernel, precision=highest) / root_rows, ROW)
    all_loadings = lax.all_gather(loadings, ROW, axis=0, tiled=True)
    deflated = kernel - jnp.dot(scores, all_loadings, precision=highest) / root_rows
    return (scores, loadings, weights, deflated, basis_next)


def solution(mesh):
    finer = Mesh(mesh.devices.reshape(4, 8, mesh.shape["col"]), ("row_0", "row_1", "col"))
    in_specs = (P(ROW, "col"), P("col", ROW), P(ROW, "col"))
    out_specs = (P(ROW, None), P(ROW, "col"), P("col", None), P(ROW, "col"), P(ROW, None))
    return jax.shard_map(local, mesh=finer, in_specs=in_specs, out_specs=out_specs, check_vma=False)
```

profile of v0, /device:TPU:8, one launch (start us, length us, event | category | flops | bytes accessed | tf_op | source)
XLA Modules:
  0.0 430.5 jit_solution(12463068032764752603)
XLA Ops:
  7.2 0.7 all-gather.5.cloned.1.call-update
  8.0 87.2 %all-gather.5.cloned.1.call-done = f32[32,4,8192]{2,1,0:T(4,128)} async-done(((f32[1,4,8192]{2,1,0:T(4,128)}), f32[32,4,8192]{2,1,0:T(4,128)}) %all-gather.5.cloned.1.call-update) | async-done | bytes 4194320 | tf_op jit(solution)/shard_map/all_gather | solution.py:33
  95.2 5.3 %reshape.25 = f32[128,8192]{1,0:T(8,128)} reshape(f32[32,4,8192]{2,1,0:T(4,128)} %all-gather.5.cloned.1.call-done) | data formatting | bytes 8388608
  100.5 6.2 %fusion.7 = f32[64,128]{1,0:T(8,128)S(1)} fusion(f32[64,8192]{1,0:T(8,128)S(1)} %copy-done.1, f32[128,8192]{1,0:T(8,128)} %reshape.25), kind=kOutput, calls=%fused_computation.19 | convolution fusion | flops 805306368 | bytes 6324224 | tf_op jit(solution)/shard_map/dot_general | solution.py:32
  106.7 10.7 %all_to_all.20 = f32[8,64,128]{2,1,0:T(8,128)S(1)} all-to-all(f32[8,64,128]{2,1,0:T(8,128)S(1)} %broadcast_in_dim.10), channel_id=1, replica_groups=mesh['row_0'=4,'row_1'=8,'col'=8] {'col'}, dimensions={0} | all-to-all | bytes 524288 | tf_op jit(solution)/shard_map/all_to_all | solution.py:13
  117.4 0.3 convolution_multiply_fusion.2
  117.7 0.2 broadcast_in_dim.11
  117.9 56.2 %all_to_all.21 = f32[32,128,128]{2,1,0:T(8,128)} all-to-all(f32[32,128,128]{2,1,0:T(8,128)S(1)} %broadcast_in_dim.11), channel_id=1, replica_groups=mesh['row_0'=4,'row_1'=8,'col'=8] {'row_0','row_1'}, dimensions={0} | all-to-all | bytes 4194304 | tf_op jit(solution)/shard_map/all_to_all | solution.py:13
  174.1 1.7 reduce_sum.37
  175.8 0.1 copy.10
  175.9 11.7 %cholesky.16 = f32[128,128]{1,0:T(8,128)S(1)} custom-call(f32[128,128]{1,0:T(8,128)S(1)} %fusion.6), custom_call_target="Cholesky" | custom-call | tf_op jit(solution)/shard_map/jit(cholesky)/cholesky | solution.py:38
  187.7 0.6 compare_reduce_fusion
  188.3 0.7 fusion.3
  189.0 9.8 %custom-call.7 = f32[1,128,128]{1,2,0:T(8,128)S(1)} custom-call(f32[1,128,128]{2,1,0:T(8,128)S(1)} %fusion.3), custom_call_target="InvertDiagBlocksLowerTriangular" | custom-call | tf_op jit(solution)/shard_map/jit(_solve_triangular)/triangular_solve | solution.py:39
  198.8 0.2 fusion.4
  199.0 5.1 %convolution_multiply_fusion = f32[128,8192]{1,0:T(8,128)} fusion(f32[128,64]{0,1:T(8,128)S(1)} %fusion.4, f32[64,8192]{1,0:T(8,128)S(1)} %copy-done.1), kind=kOutput, calls=%fused_computation | convolution fusion | flops 806354944 | bytes 6324224 | tf_op jit(solution)/shard_map/dot_general | solution.py:44
  204.1 0.0 all-reduce.3.cloned.1.call-start
  204.1 45.0 %reduce-scatter.2.cloned.1.call-done = f32[32,8192]{1,0:T(8,128)} async-done(((f32[128,8192]{1,0:T(8,128)}), f32[32,8192]{1,0:T(8,128)}) %reduce-scatter.2.cloned.1.call-update) | async-done | bytes 1048592 | tf_op jit(solution)/shard_map/reduce_scatter | solution.py:23
  249.2 0.6 dynamic-slice
  250.4 76.9 %all-reduce.3.cloned.1.call-done = f32[32,8192]{1,0:T(8,128)} async-done(((f32[32,8192]{1,0:T(8,128)}), f32[32,8192]{1,0:T(8,128)}) %all-reduce.3.cloned.1.call-update) | async-done | bytes 1048592
  327.3 1.6 fusion.21
  328.9 0.2 fusion.2
  329.2 0.1 broadcast_in_dim.12
  329.3 33.8 %all_to_all.22 = f32[32,64,128]{2,1,0:T(8,128)S(1)} all-to-all(f32[32,64,128]{2,1,0:T(8,128)S(1)} %broadcast_in_dim.12), channel_id=1, replica_groups=mesh['row_0'=4,'row_1'=8,'col'=8] {'row_0','row_1'}, dimensions={0} | all-to-all | bytes 2097152 | tf_op jit(solution)/shard_map/all_to_all | solution.py:13
  363.1 0.1 reduce_sum.38
  363.2 0.2 fusion.1
  363.4 10.7 %all_to_all.23 = f32[8,64,128]{2,1,0:T(8,128)S(1)} all-to-all(f32[8,64,128]{2,1,0:T(8,128)S(1)} %broadcast_in_dim.13), channel_id=1, replica_groups=mesh['row_0'=4,'row_1'=8,'col'=8] {'col'}, dimensions={0} | all-to-all | bytes 524288 | tf_op jit(solution)/shard_map/all_to_all | solution.py:13
  374.1 0.6 reduce_sum.39
  374.7 1.6 constant_dynamic-slice_fusion
  376.4 36.4 %all-gather.7.cloned.1.call-done = f32[32,4,8192]{2,1,0:T(4,128)} async-done(((f32[1,4,8192]{2,1,0:T(4,128)}), f32[32,4,8192]{2,1,0:T(4,128)}) %all-gather.7.cloned.1.call-update) | async-done | bytes 4194320 | tf_op jit(solution)/shard_map/all_gather | solution.py:45
  412.8 5.3 %reshape.27 = f32[128,8192]{1,0:T(8,128)} reshape(f32[32,4,8192]{2,1,0:T(4,128)} %all-gather.7.cloned.1.call-done) | data formatting | bytes 8388608
  418.1 5.9 %fusion = f32[64,8192]{1,0:T(8,128)} fusion(f32[64,8192]{1,0:T(8,128)S(1)} %copy-done.1, f32[128,64]{0,1:T(8,128)S(1)} %fusion.4, f32[128,8192]{1,0:T(8,128)} %reshape.27), kind=kOutput, calls=%fused_computation.2 | convolution fusion | flops 806354944 | bytes 8421376 | tf_op jit(solution)/shard_map/dot_general | solution.py:46
  (21 shorter events, 0.3 us)
Async XLA Ops:
  7.2 321.8 %copy-start = (f32[64,64]{1,0:T(8,128)S(1)}, f32[64,64]{1,0:T(8,128)}, u32[]{:S(2)}) copy-start(f32[64,64]{1,0:T(8,128)} %param.5) | copy-start | bytes 49156
  7.2 88.0 %all-gather.5.cloned.1.call-start = ((), (), s32[]{:S(2)}) async-start(), calls=%async_computation.6 | async-start | bytes 4325376 | tf_op jit(solution)/shard_map/all_gather | solution.py:33
  7.9 92.6 %copy-start.1 = (f32[64,8192]{1,0:T(8,128)S(1)}, f32[64,8192]{1,0:T(8,128)}, u32[]{:S(2)}) copy-start(f32[64,8192]{1,0:T(8,128)} %param.3) | copy-start | bytes 6291460
  7.9 241.2 %reduce-scatter.2.cloned.1.call-start = ((), (), s32[]{:S(2)}) async-start(), calls=%async_computation.5 | async-start | bytes 5242880 | tf_op jit(solution)/shard_map/reduce_scatter | solution.py:23
  199.0 219.1 %copy-start.2 = (f32[128,64]{0,1:T(8,128)}, f32[128,64]{0,1:T(8,128)S(1)}, u32[]{:S(2)}) copy-start(f32[128,64]{0,1:T(8,128)S(1)} %fusion.4) | copy-start | bytes 98308
  204.1 45.1 %copy-start.4 = (u32[256]{0:T(256)S(1)}, u32[256]{0:T(256)}, u32[]{:S(2)}) copy-start(u32[256]{0:T(256)} %constant.60) | copy-start | bytes 3076
  204.1 123.2 %all-reduce.3.cloned.1.call-start = ((), (), s32[]{:S(2)}) async-start(), calls=%async_computation.8 | async-start | bytes 2097152
  249.1 163.7 %all-gather.7.cloned.1.call-start = ((), (), s32[]{:S(2)}) async-start(), calls=%async_computation.7 | async-start | bytes 4325376 | tf_op jit(solution)/shard_map/all_gather | solution.py:45
  363.2 54.9 %copy-start.3 = (f32[64,128]{1,0:T(8,128)}, f32[64,128]{1,0:T(8,128)S(1)}, u32[]{:S(2)}) copy-start(f32[64,128]{1,0:T(8,128)S(1)} %reduce_sum.38) | copy-start | bytes 98308
Sparse Core Ops, SparseCore 0:
  10.6 84.5 all-gather.4
  204.2 44.8 reduce-scatter.1
  251.4 75.7 all-reduce.2
  330.3 82.4 all-gather.6
where the time goes:
time: 431 us; the launch traced here: 430 us
  waiting for transfers between devices  246 us (57%)
  blocking collectives  111 us (26%)
  other arithmetic  25.3 us (6%)
  matrix products  18 us (4%)
  local copies, waits for them, and re-layouts  14.9 us (3%)
  between operations  14.6 us (3%)
    all_to_all x4, blocking collectives, sent_to_all(): lax.all_to_all(jnp.broadcast_to(x[None], (devices, *x.shape)), axis, 0, 0...  111 us
    all_gather x1, waiting for transfers between devices, local(): lax.all_gather(basis, ROW, axis=1, tiled=True)  87.2 us
    unnamed x5, waiting for transfers between devices  77.6 us
    reduce_scatter x1, waiting for transfers between devices, summed_rows(): subtotal = lax.psum_scatter(subtotal, axis, scatter_dimension=0, tiled=True)  45 us
    all_gather x1, waiting for transfers between devices, local(): all_loadings = lax.all_gather(loadings, ROW, axis=0, tiled=True)  36.4 us
    unnamed x15, local copies, waits for them, and re-layouts  14.4 us
    another operation x3, other arithmetic, local(): factor = jnp.linalg.cholesky(gram_mat)  12.4 us
    another operation x2, other arithmetic, local(): jax.scipy.linalg.solve_triangular(factor, projected.T, lower=True)  10.5 us
  transfers between devices with their start and end apart: 4, of which 4 were waited for; matrix products, arithmetic and copies ran while one was open for 1% of the time, Pallas kernels for 0%

commit v1 on v0

--- a/solution.py
+++ b/solution.py
@@ -42,7 +42,10 @@
     next_part = jnp.dot(responses, weights, precision=highest) / math.sqrt(resp_count)
     basis_next = taken_together(next_part, "col")
     loadings = summed_rows(jnp.dot(scores.T, kernel, precision=highest) / root_rows, ROW)
-    all_loadings = lax.all_gather(loadings, ROW, axis=0, tiled=True)
+    supply_all_members_all = lambda content: jnp.concatenate(
+        lax.all_to_all(jnp.stack(lax.axis_size(ROW) * [content], 0), ROW, 0, 0), 0
+    )
+    all_loadings = supply_all_members_all(loadings)
     deflated = kernel - jnp.dot(scores, all_loadings, precision=highest) / root_rows
     return (scores, loadings, weights, deflated, basis_next)
 

time: 431 us -> 458 us (1.063)
  waiting for transfers between devices: 246 us -> 299 us
  blocking collectives: 111 us -> 66.8 us
  starting transfers between devices: 0.16 us -> 16.7 us
    all_to_all x0 -> x3, waiting for transfers between devices: none -> 91.5 us  [the longest x1 91.5 us: local(): lax.all_to_all(jnp.stack(lax.axis_size(ROW) * [content], 0), ROW, 0, 0)]
    all_to_all x4 -> x2, blocking collectives: 111 us -> 66.8 us  [sent_to_all(): lax.all_to_all(jnp.broadcast_to(x[None], (devices, *x.shape)), axis, 0, 0...]
    all_gather x1 -> x0, waiting for transfers between devices: 36.4 us -> none  [local(): all_loadings = lax.all_gather(loadings, ROW, axis=0, tiled=True)]
    all_to_all x0 -> x3, starting transfers between devices: none -> 16.6 us  [the longest x2 9.49 us: sent_to_all(): lax.all_to_all(jnp.broadcast_to(x[None], (devices, *x.shape)), axis, 0, 0...]
    unnamed x15, local copies, waits for them, and re-layouts: 14.4 us -> 6.88 us
    unnamed x5 -> x4, waiting for transfers between devices: 77.6 us -> 71 us
    reshape x0 -> x1, local copies, waits for them, and re-layouts: none -> 5.28 us  [local(): jnp.concatenate(lax.all_to_all(jnp.stack(lax.axis_size(ROW) * [content],...]
  transfers between devices with their start and end apart: 4 -> 6, of which waited for: 4 -> 4; matrix products, arithmetic and copies ran while one was open for 1% -> 1% of each run, Pallas kernels for 0% -> 0%
where the time goes in v1:
time: 458 us
  waiting for transfers between devices  299 us (65%)
  blocking collectives  66.8 us (15%)
  other arithmetic  25.3 us (6%)
  matrix products  18 us (4%)
  local copies, waits for them, and re-layouts  17.2 us (4%)
  starting transfers between devices  16.7 us (4%)
  between operations  14.6 us (3%)
    all_to_all x1, waiting for transfers between devices, local(): lax.all_to_all(jnp.stack(lax.axis_size(ROW) * [content], 0), ROW, 0, 0)  91.5 us
    all_gather x1, waiting for transfers between devices, local(): lax.all_gather(basis, ROW, axis=1, tiled=True)  87.2 us
    unnamed x4, waiting for transfers between devices  71 us
    all_to_all x2, blocking collectives, sent_to_all(): lax.all_to_all(jnp.broadcast_to(x[None], (devices, *x.shape)), axis, 0, 0...  66.8 us
    reduce_scatter x1, waiting for transfers between devices, summed_rows(): subtotal = lax.psum_scatter(subtotal, axis, scatter_dimension=0, tiled=True)  49.4 us
    another operation x3, other arithmetic, local(): factor = jnp.linalg.cholesky(gram_mat)  12.4 us
    another operation x2, other arithmetic, local(): jax.scipy.linalg.solve_triangular(factor, projected.T, lower=True)  10.5 us
    all_to_all x2, starting transfers between devices, sent_to_all(): lax.all_to_all(jnp.broadcast_to(x[None], (devices, *x.shape)), axis, 0, 0...  9.49 us
  transfers between devices with their start and end apart: 6, of which 4 were waited for; matrix products, arithmetic and copies ran while one was open for 1% of the time, Pallas kernels for 0%

profile of v1, /device:TPU:8, one launch (start us, length us, event | category | flops | bytes accessed | tf_op | source)
XLA Modules:
  0.0 457.8 jit_solution(15297981898058067649)
XLA Ops:
  7.2 0.7 all-gather.3.cloned.1.call-update
  8.0 87.2 %all-gather.3.cloned.1.call-done = f32[32,4,8192]{2,1,0:T(4,128)} async-done(((f32[1,4,8192]{2,1,0:T(4,128)}), f32[32,4,8192]{2,1,0:T(4,128)}) %all-gather.3.cloned.1.call-update) | async-done | bytes 4194320 | tf_op jit(solution)/shard_map/all_gather | solution.py:33
  95.2 5.3 %reshape.31 = f32[128,8192]{1,0:T(8,128)} reshape(f32[32,4,8192]{2,1,0:T(4,128)} %all-gather.3.cloned.1.call-done) | data formatting | bytes 8388608
  100.5 6.2 %fusion.7 = f32[64,128]{1,0:T(8,128)S(1)} fusion(f32[64,8192]{1,0:T(8,128)S(1)} %copy-done.1, f32[128,8192]{1,0:T(8,128)} %reshape.31), kind=kOutput, calls=%fused_computation.19 | convolution fusion | flops 805306368 | bytes 6324224 | tf_op jit(solution)/shard_map/dot_general | solution.py:32
  106.7 10.7 %all_to_all.25 = f32[8,64,128]{2,1,0:T(8,128)S(1)} all-to-all(f32[8,64,128]{2,1,0:T(8,128)S(1)} %broadcast_in_dim.10), channel_id=1, replica_groups=mesh['row_0'=4,'row_1'=8,'col'=8] {'col'}, dimensions={0} | all-to-all | bytes 524288 | tf_op jit(solution)/shard_map/all_to_all | solution.py:13
  117.4 0.3 convolution_multiply_fusion.2
  117.7 0.2 broadcast_in_dim.11
  117.9 56.2 %all_to_all.26 = f32[32,128,128]{2,1,0:T(8,128)} all-to-all(f32[32,128,128]{2,1,0:T(8,128)S(1)} %broadcast_in_dim.11), channel_id=1, replica_groups=mesh['row_0'=4,'row_1'=8,'col'=8] {'row_0','row_1'}, dimensions={0} | all-to-all | bytes 4194304 | tf_op jit(solution)/shard_map/all_to_all | solution.py:13
  174.1 1.7 reduce_sum.37
  175.8 0.1 copy.10
  175.9 11.7 %cholesky.16 = f32[128,128]{1,0:T(8,128)S(1)} custom-call(f32[128,128]{1,0:T(8,128)S(1)} %fusion.6), custom_call_target="Cholesky" | custom-call | tf_op jit(solution)/shard_map/jit(cholesky)/cholesky | solution.py:38
  187.7 0.6 compare_reduce_fusion
  188.3 0.7 fusion.3
  189.0 9.8 %custom-call.7 = f32[1,128,128]{1,2,0:T(8,128)S(1)} custom-call(f32[1,128,128]{2,1,0:T(8,128)S(1)} %fusion.3), custom_call_target="InvertDiagBlocksLowerTriangular" | custom-call | tf_op jit(solution)/shard_map/jit(_solve_triangular)/triangular_solve | solution.py:39
  198.8 0.2 fusion.4
  199.0 5.1 %convolution_multiply_fusion = f32[128,8192]{1,0:T(8,128)} fusion(f32[128,64]{0,1:T(8,128)S(1)} %fusion.4, f32[64,8192]{1,0:T(8,128)S(1)} %copy-done.1), kind=kOutput, calls=%fused_computation | convolution fusion | flops 806354944 | bytes 6324224 | tf_op jit(solution)/shard_map/dot_general | solution.py:44
  204.1 0.2 fusion.2
  204.3 1.1 broadcast_in_dim.12
  205.4 4.9 %all-to-all-start.2 = ((f32[32,64,128]{2,1,0:T(8,128)}), f32[32,64,128]{2,1,0:T(8,128)S(1)}, u32[]{:S(2)}, u32[]{:S(2)}) async-start(f32[32,64,128]{2,1,0:T(8,128)} %broadcast_in_dim.12), calls=%async_computation.3 | async-start | bytes 2097152 | tf_op jit(solution)/shard_map/all_to_all | solution.py:13
  210.4 49.4 %reduce-scatter.2.cloned.1.call-done = f32[32,8192]{1,0:T(8,128)} async-done(((f32[128,8192]{1,0:T(8,128)}), f32[32,8192]{1,0:T(8,128)}) %reduce-scatter.2.cloned.1.call-update) | async-done | bytes 1048592 | tf_op jit(solution)/shard_map/reduce_scatter | solution.py:23
  259.9 0.6 dynamic-slice
  261.2 0.2 fusion.1
  261.4 0.7 broadcast_in_dim.13
  262.1 4.6 all-to-all-start.4
  266.7 70.3 %all-reduce.3.cloned.1.call-done = f32[32,8192]{1,0:T(8,128)} async-done(((f32[32,8192]{1,0:T(8,128)}), f32[32,8192]{1,0:T(8,128)}) %all-reduce.3.cloned.1.call-update) | async-done | bytes 1048592
  336.9 1.0 constant_dynamic-slice_fusion
  337.9 2.9 stack.2
  340.9 7.1 %all-to-all-start.3 = ((f32[32,4,8192]{2,1,0:T(4,128)}), f32[32,4,8192]{2,1,0:T(4,128)}, u32[]{:S(2)}, u32[]{:S(2)}) async-start(f32[32,4,8192]{2,1,0:T(4,128)} %stack.2), calls=%async_computation.4 | async-start | bytes 8388608 | tf_op jit(solution)/shard_map/all_to_all | solution.py:46
  348.0 0.6 reduce_sum.39
  348.6 91.5 %all-to-all-done.3 = f32[32,4,8192]{2,1,0:T(4,128)} async-done(((f32[32,4,8192]{2,1,0:T(4,128)}), f32[32,4,8192]{2,1,0:T(4,128)}, u32[]{:S(2)}, u32[]{:S(2)}) %all-to-all-start.3) | async-done | bytes 4194336 | tf_op jit(solution)/shard_map/all_to_all | solution.py:46
  440.1 5.3 %reshape.29 = f32[128,8192]{1,0:T(8,128)} reshape(f32[32,4,8192]{2,1,0:T(4,128)} %all-to-all-done.3) | data formatting | bytes 8388608 | tf_op jit(solution)/shard_map/reshape | solution.py:45
  445.4 5.9 %fusion = f32[64,8192]{1,0:T(8,128)} fusion(f32[64,8192]{1,0:T(8,128)S(1)} %copy-done.1, f32[128,64]{0,1:T(8,128)S(1)} %fusion.4, f32[128,8192]{1,0:T(8,128)} %reshape.29), kind=kOutput, calls=%fused_computation.2 | convolution fusion | flops 806354944 | bytes 8421376 | tf_op jit(solution)/shard_map/dot_general | solution.py:49
  (24 shorter events, 0.3 us)
Async XLA Ops:
  7.2 196.9 %copy-start = (f32[64,64]{1,0:T(8,128)S(1)}, f32[64,64]{1,0:T(8,128)}, u32[]{:S(2)}) copy-start(f32[64,64]{1,0:T(8,128)} %param.5) | copy-start | bytes 49156
  7.2 88.0 %all-gather.3.cloned.1.call-start = ((), (), s32[]{:S(2)}) async-start(), calls=%async_computation.7 | async-start | bytes 4325376 | tf_op jit(solution)/shard_map/all_gather | solution.py:33
  7.9 92.6 %copy-start.1 = (f32[64,8192]{1,0:T(8,128)S(1)}, f32[64,8192]{1,0:T(8,128)}, u32[]{:S(2)}) copy-start(f32[64,8192]{1,0:T(8,128)} %param.3) | copy-start | bytes 6291460
  7.9 251.9 %reduce-scatter.2.cloned.1.call-start = ((), (), s32[]{:S(2)}) async-start(), calls=%async_computation.6 | async-start | bytes 5242880 | tf_op jit(solution)/shard_map/reduce_scatter | solution.py:23
  199.0 246.4 %copy-start.2 = (f32[128,64]{0,1:T(8,128)}, f32[128,64]{0,1:T(8,128)S(1)}, u32[]{:S(2)}) copy-start(f32[128,64]{0,1:T(8,128)S(1)} %fusion.4) | copy-start | bytes 98308
  204.1 55.8 %copy-start.5 = (u32[256]{0:T(256)S(1)}, u32[256]{0:T(256)}, u32[]{:S(2)}) copy-start(u32[256]{0:T(256)} %constant.60) | copy-start | bytes 3076
  205.4 55.7 %all-to-all-start.2 = ((f32[32,64,128]{2,1,0:T(8,128)}), f32[32,64,128]{2,1,0:T(8,128)S(1)}, u32[]{:S(2)}, u32[]{:S(2)}) async-start(f32[32,64,128]{2,1,0:T(8,128)} %broadcast_in_dim.12), calls=%async_computation.3 | async-start | bytes 2097152 | tf_op jit(solution)/shard_map/all_to_all | solution.py:13
  210.4 126.6 %all-reduce.3.cloned.1.call-start = ((), (), s32[]{:S(2)}) async-start(), calls=%async_computation.8 | async-start | bytes 2097152
  261.2 79.6 %copy-start.4 = (f32[64,128]{1,0:T(8,128)}, f32[64,128]{1,0:T(8,128)S(1)}, u32[]{:S(2)}) copy-start(f32[64,128]{1,0:T(8,128)S(1)} %reduce_sum.38) | copy-start | bytes 98308
  262.1 75.8 %all-to-all-start.4 = ((f32[8,64,128]{2,1,0:T(8,128)}), f32[8,64,128]{2,1,0:T(8,128)S(1)}, u32[]{:S(2)}, u32[]{:S(2)}) async-start(f32[8,64,128]{2,1,0:T(8,128)} %broadcast_in_dim.13), calls=%async_computation.5 | async-start | bytes 524288 | tf_op jit(solution)/shard_map/all_to_all | solution.py:13
  337.9 2.9 copy-start.3
  340.9 99.2 %all-to-all-start.3 = ((f32[32,4,8192]{2,1,0:T(4,128)}), f32[32,4,8192]{2,1,0:T(4,128)}, u32[]{:S(2)}, u32[]{:S(2)}) async-start(f32[32,4,8192]{2,1,0:T(4,128)} %stack.2), calls=%async_computation.4 | async-start | bytes 8388608 | tf_op jit(solution)/shard_map/all_to_all | solution.py:46
Sparse Core Ops, SparseCore 0:
  10.6 84.5 all-gather.2
  204.2 55.5 reduce-scatter.1
  262.2 74.6 all-reduce.2
